TPU v7x, 32 devices: a whole 2x2x4 slice. The times are simulated.
32 devices in a mesh: tm: 8 (over z, x), state: 4 (over y, core).
Axes of the slice: x: 2, y: 2, z: 4, core: 2. Of those that a mesh axis runs over, the one named last changes fastest.
Arguments:
- trans_weight: bfloat16 [8, 2048, 2048], P('tm', None, 'state'), may hold values from 6e-06 to 163000
- pattern: int32 [16, 16], replicated, may hold values 0 or 1
- boundary: int32 [8], P('tm'), may hold values 0 or 1
- log_emit: float32 [8, 2048], P('tm', 'state'), may hold values from -63 to 153
Outputs:
- quad_op: float32 [4096, 2048], P('tm', 'state')
All inputs are finite; a program needn't handle non-finite values. No bound on the sum of `boundary` on one device may be relied on, other than what follows from the above.
Results may differ from a plain program's by a relative error of at most 0.0003.
Values sent between devices are 32-bit elements; how exact they have to be, the bound alone decides.
A program may use at most 64 MiB of HBM per device.

v0:
```python
import jax
import jax.numpy as jnp
from jax import lax
from jax.sharding import PartitionSpec as P

BLOCK = 128


def from_partner(shard, axis, apart):
    return lax.ppermute(shard, axis, [(i, i ^ 1 << apart) for i in range(lax.axis_size(axis))])


def block_mask(pattern, row_count, col_start, col_count):
    block_count = pattern.shape[0]
    row_ids = jnp.arange(row_count, dtype=jnp.int32) // BLOCK
    col_ids = (col_start + jnp.arange(col_count, dtype=jnp.int32)) // BLOCK
    blocks = jnp.arange(block_count, dtype=jnp.int32)
    row_hot = (row_ids[:, None] == blocks[None, :]).astype(jnp.float32)
    col_hot = (blocks[:, None] == col_ids[None, :]).astype(jnp.float32)
    lookup = pattern.astype(jnp.float32)
    return jnp.dot(jnp.dot(row_hot, lookup), col_hot)


def combine(left_log, right_log):
    row_top = jnp.max(left_log, axis=1, keepdims=True)
    col_top = jnp.max(right_log, axis=0, keepdims=True)
    lead = jnp.exp(left_log - row_top).astype(jnp.bfloat16)
    trail = jnp.exp(right_log - col_top).astype(jnp.bfloat16)
    summed = jnp.dot(lead, trail, preferred_element_type=jnp.float32)
    return row_top + col_top + jnp.log(summed)


def on_device(trans_weight, pattern, boundary, log_emit):
    weight = trans_weight[0]
    states, col_width = weight.shape
    col_start = lax.axis_index("state") * col_width
    restart = 0.0001 + 0.4999 * boundary.astype(jnp.float32)
    mask_table = block_mask(pattern, states, col_start, col_width)
    mixture = (1.0 - restart) * (4.0 / states) * weight.astype(
        jnp.float32
    ) * mask_table + restart / states
    own_op = jnp.log(mixture) + log_emit
    tm_index = lax.axis_index("tm")
    half_index = tm_index % 2
    partner_op = from_partner(own_op, "tm", 0)
    first_op = jnp.where(half_index == 0, own_op, partner_op)
    second_op = jnp.where(half_index == 0, partner_op, own_op)
    row_start = half_index * (states // 2)
    row_count = states // 2
    left_slab = lax.dynamic_slice_in_dim(first_op, row_start, row_count, 0)
    left_full = lax.all_gather(left_slab, "state", axis=1, tiled=True)
    pair_op = combine(left_full, second_op)
    other_half = from_partner(pair_op, "tm", 0)
    own_pair = jnp.where(
        half_index == 0,
        jnp.concatenate([pair_op, other_half], axis=0),
        jnp.concatenate([other_half, pair_op], axis=0),
    )
    other_pair = from_partner(own_pair, "tm", 1)
    leading = tm_index // 2 % 2 == 0
    quarter = states // 4
    quarter_start = tm_index % 4 * quarter
    own_rows = lax.dynamic_slice_in_dim(own_pair, quarter_start, quarter, 0)
    other_rows = lax.dynamic_slice_in_dim(other_pair, quarter_start, quarter, 0)
    quad_slab = jnp.where(leading, own_rows, other_rows)
    right_pair = jnp.where(leading, other_pair, own_pair)
    quad_left = lax.all_gather(quad_slab, "state", axis=1, tiled=True)
    return combine(quad_left, right_pair)


def solution(mesh):
    return jax.shard_map(
        on_device,
        mesh=mesh,
        in_specs=(P("tm", None, "state"), P(), P("tm"), P("tm", "state")),
        out_specs=P("tm", "state"),
        check_vma=False,
    )
```

profile of v0, /device:TPU:0, one launch (start us, length us, event | category | flops | bytes accessed | tf_op | source)
XLA Modules:
  0.0 375.7 jit_solution(6337932703887638775)
XLA Ops:
  6.5 0.0 all-gather.3.cloned.1.call-start
  7.2 5.0 %fusion.3 = f32[2048,512]{1,0:T(8,128)} fusion(bf16[1,2048,512]{2,1,0:T(8,128)(2,1)} %param.4, f32[512]{0:T(512)} %bitcast.11, f32[]{:T(128)} %bitcast.2, f32[]{:T(128)} %bitcast, s32[2048]{0:T(1024)S(1)} %add_select_fusion, s32[512]{0:T(512)S(1)} %add_select_fusion.1, s32[16,16]{1,0:T(8,128)} %param.5), kind=kOutput, calls=%fused_computation.6 | convolution fusion | flops 39887104 | bytes 6304776 | tf_op jit(solution)/shard_map/dot_general | solution.py:21
  12.2 2.9 collective-permute-start
  15.1 90.9 %collective-permute-done = f32[2048,512]{1,0:T(8,128)} collective-permute-done((f32[2048,512]{1,0:T(8,128)}, f32[2048,512]{1,0:T(8,128)}, u32[]{:S(2)}, u32[]{:S(2)}) %collective-permute-start) | collective-permute-done | bytes 4194336 | tf_op jit(solution)/shard_map/ppermute | solution.py:10
  106.0 4.0 %dynamic-slice_select_fusion = f32[1024,512]{1,0:T(8,128)} fusion(f32[2048,512]{1,0:T(8,128)} %collective-permute-done, s32[]{:T(128)S(6)} %select_n.82, f32[2048,512]{1,0:T(8,128)} %fusion.3, pred[]{:T(512)S(6)} %eq.39), kind=kLoop, calls=%fused_computation.12 | loop fusion | flops 524288 | bytes 6291461 | tf_op jit(solution)/shard_map/jit(_where)/select_n | solution.py:46
  110.1 0.0 all-gather.3.cloned.1.call-update
  110.1 0.0 all-gather.5.cloned.1.call-start
  110.1 2.7 fusion.9
  112.8 57.2 %all-gather.3.cloned.1.call-done = f32[1024,2048]{1,0:T(8,128)} async-done(((f32[1024,512]{1,0:T(8,128)}), f32[1024,2048]{1,0:T(8,128)}) %all-gather.3.cloned.1.call-update) | async-done | bytes 8388624 | tf_op jit(solution)/shard_map/all_gather | solution.py:51
  170.0 3.8 %reduce_max.36 = f32[1024]{0:T(1024)S(1)} reduce(f32[1024,2048]{1,0:T(8,128)} %all-gather.3.cloned.1.call-done, f32[]{:T(128)} %constant.88.clone.1), dimensions={1}, to_apply=%region_0.1 | reduce | flops 2096128 | bytes 8392708 | tf_op jit(solution)/shard_map/reduce_max | solution.py:25
  173.9 6.5 %log_add_fusion = f32[1024,512]{1,0:T(8,128)S(1)} fusion(f32[512]{0:T(512)S(1)} %fusion.9, f32[2048,512]{1,0:T(8,128)} %collective-permute-done, f32[2048,512]{1,0:T(8,128)} %fusion.3, pred[]{:T(512)S(6)} %eq.39, f32[1024,2048]{1,0:T(8,128)} %all-gather.3.cloned.1.call-done, f32[1024]{0:T(1024)S(1)} %reduce_max.36), kind=kOutput, calls=%fused_computation.15 | convolution fusion | flops 2155872256 | bytes 18880512 | tf_op jit(solution)/shard_map/dot_general | solution.py:29
  180.3 1.5 collective-permute-start.1
  181.9 46.3 %collective-permute-done.1 = f32[1024,512]{1,0:T(8,128)S(1)} collective-permute-done((f32[1024,512]{1,0:T(8,128)S(1)}, f32[1024,512]{1,0:T(8,128)S(1)}, u32[]{:S(2)}, u32[]{:S(2)}) %collective-permute-start.1) | collective-permute-done | bytes 2097184 | tf_op jit(solution)/shard_map/ppermute | solution.py:10
  228.2 2.8 maximum_select_fusion
  231.0 1.5 collective-permute-start.2
  232.5 90.8 %collective-permute-done.2 = f32[2048,512]{1,0:T(8,128)} collective-permute-done((f32[2048,512]{1,0:T(8,128)}, f32[2048,512]{1,0:T(8,128)}, u32[]{:S(2)}, u32[]{:S(2)}) %collective-permute-start.2) | collective-permute-done | bytes 4194336 | tf_op jit(solution)/shard_map/ppermute | solution.py:10
  323.3 2.7 dynamic-slice_select_fusion.1
  326.0 0.0 all-gather.5.cloned.1.call-update
  326.0 2.7 fusion.10
  328.7 31.9 %all-gather.5.cloned.1.call-done = f32[512,2048]{1,0:T(8,128)} async-done(((f32[512,512]{1,0:T(8,128)}), f32[512,2048]{1,0:T(8,128)}) %all-gather.5.cloned.1.call-update) | async-done | bytes 4194320 | tf_op jit(solution)/shard_map/all_gather | solution.py:67
  360.6 2.5 reduce_max.38
  363.1 5.8 %add_add_fusion = f32[512,512]{1,0:T(8,128)} fusion(f32[512]{0:T(512)S(1)} %fusion.10, f32[512]{0:T(512)S(1)} %reduce_max.38, f32[2048,512]{1,0:T(8,128)} %collective-permute-done.2, f32[2048,512]{1,0:T(8,128)} %maximum_select_fusion, pred[]{:T(512)S(6)} %eq.38, f32[512,2048]{1,0:T(8,128)} %all-gather.5.cloned.1.call-done), kind=kOutput, calls=%fused_computation.23 | convolution fusion | flops 1079508992 | bytes 13635585 | tf_op jit(solution)/shard_map/dot_general | solution.py:29
  (2 shorter events, 0.0 us)
Async XLA Ops:
  6.5 163.5 %all-gather.3.cloned.1.call-start = ((), (), s32[]{:S(2)}) async-start(), calls=%async_computation | async-start | bytes 10485760 | tf_op jit(solution)/shard_map/all_gather | solution.py:51
  12.2 93.8 %collective-permute-start = (f32[2048,512]{1,0:T(8,128)}, f32[2048,512]{1,0:T(8,128)}, u32[]{:S(2)}, u32[]{:S(2)}) collective-permute-start(f32[2048,512]{1,0:T(8,128)} %fusion.3), channel_id=1, source_target_pairs={{0,4},{4,0},{8,12},{12,8},{16,20},{20,16},{24,28},{28,24},{1,5},{5... | collective-permute-start | bytes 12582920 | tf_op jit(solution)/shard_map/ppermute | solution.py:10
  110.1 250.6 %all-gather.5.cloned.1.call-start = ((), (), s32[]{:S(2)}) async-start(), calls=%async_computation.1 | async-start | bytes 5242880 | tf_op jit(solution)/shard_map/all_gather | solution.py:67
  180.3 47.9 %collective-permute-start.1 = (f32[1024,512]{1,0:T(8,128)S(1)}, f32[1024,512]{1,0:T(8,128)S(1)}, u32[]{:S(2)}, u32[]{:S(2)}) collective-permute-start(f32[1024,512]{1,0:T(8,128)S(1)} %log_add_fusion), channel_id=1, source_target_pairs={{0,4},{4,0},{8,12},{12,8},{16,20},{20,16},{24,28},{28,24},{1,5},{5... | collective-permute-start | bytes 6291464 | tf_op jit(solution)/shard_map/ppermute | solution.py:10
  231.0 92.2 %collective-permute-start.2 = (f32[2048,512]{1,0:T(8,128)}, f32[2048,512]{1,0:T(8,128)}, u32[]{:S(2)}, u32[]{:S(2)}) collective-permute-start(f32[2048,512]{1,0:T(8,128)} %maximum_select_fusion), channel_id=1, source_target_pairs={{0,8},{4,12},{8,0},{12,4},{16,24},{20,28},{24,16},{28,20},{1,9},{5... | collective-permute-start | bytes 12582920 | tf_op jit(solution)/shard_map/ppermute | solution.py:10
Sparse Core Ops, SparseCore 0:
  110.2 59.7 all-gather.2
  326.1 34.4 all-gather.4
where the time goes:
time: 376 us
  waiting for transfers between devices  317 us (84%)
  other arithmetic  21.3 us (6%)
  matrix products  17.2 us (5%)
  between operations  14.1 us (4%)
  starting transfers between devices  6 us (2%)
    ppermute x3, waiting for transfers between devices, from_partner(): lax.ppermute(shard, axis, [(i, i ^ 1 << apart) for i in range(lax.axis_si...  228 us
    all_gather x1, waiting for transfers between devices, on_device(): left_full = lax.all_gather(left_slab, 'state', axis=1, tiled=True)  57.2 us
    all_gather x1, waiting for transfers between devices, on_device(): quad_left = lax.all_gather(quad_slab, 'state', axis=1, tiled=True)  31.9 us
    dot_general x2, matrix products, combine(): summed = jnp.dot(lead, trail, preferred_element_type=jnp.float32)  12.3 us
  transfers between devices with their start and end apart: 5, of which 5 were waited for; matrix products, arithmetic and copies ran while one was open for 1% of the time, Pallas kernels for 0%

commit v1 on v0

--- a/solution.py
+++ b/solution.py
@@ -4,6 +4,24 @@
 from jax.sharding import PartitionSpec as P
 
 BLOCK = 128
+
+
+def laid_out(blocks, dim):
+    dims = list(blocks.shape[1:])
+    dims[dim] *= blocks.shape[0]
+    return jnp.moveaxis(blocks, 0, dim).reshape(dims)
+
+
+def doubled(array, axis):
+    size = lax.axis_size(axis)
+    blocks = array[None]
+    for level in range(size.bit_length() - 1):
+        bit = 1 << level
+        other = lax.ppermute(blocks, axis, [(i, i ^ bit) for i in range(size)])
+        both = jnp.stack([blocks, other])
+        upper = lax.axis_index(axis) >> level & 1
+        blocks = jnp.where(upper == 0, both, both[::-1]).reshape(-1, *array.shape)
+    return blocks
 
 
 def from_partner(shard, axis, apart):
@@ -48,7 +66,7 @@
     row_start = half_index * (states // 2)
     row_count = states // 2
     left_slab = lax.dynamic_slice_in_dim(first_op, row_start, row_count, 0)
-    left_full = lax.all_gather(left_slab, "state", axis=1, tiled=True)
+    left_full = laid_out(doubled(left_slab, "state"), 1)
     pair_op = combine(left_full, second_op)
     other_half = from_partner(pair_op, "tm", 0)
     own_pair = jnp.where(

time: 376 us -> 421 us (1.12)
  waiting for transfers between devices: 317 us -> 353 us
  other arithmetic: 21.3 us -> 29.8 us
    ppermute x0 -> x2, waiting for transfers between devices: none -> 92.9 us  [doubled(): other = lax.ppermute(blocks, axis, [(i, i ^ bit) for i in range(size)])]
    all_gather x1 -> x0, waiting for transfers between devices: 57.2 us -> none  [on_device(): left_full = lax.all_gather(left_slab, 'state', axis=1, tiled=True)]
    another operation x0 -> x4, other arithmetic: none -> 13.8 us  [doubled(): both = jnp.stack([blocks, other])]
  transfers between devices with their start and end apart: 5 -> 6, of which waited for: 5 -> 6; matrix products, arithmetic and copies ran while one was open for 1% -> 1% of each run, Pallas kernels for 0% -> 0%
where the time goes in v1:
time: 421 us
  waiting for transfers between devices  353 us (84%)
  other arithmetic  29.8 us (7%)
  matrix products  14.1 us (3%)
  between operations  14.1 us (3%)
  starting transfers between devices  6.57 us (2%)
    ppermute x3, waiting for transfers between devices, from_partner(): lax.ppermute(shard, axis, [(i, i ^ 1 << apart) for i in range(lax.axis_si...  227 us
    ppermute x2, waiting for transfers between devices, doubled(): other = lax.ppermute(blocks, axis, [(i, i ^ bit) for i in range(size)])  92.9 us
    all_gather x1, waiting for transfers between devices, on_device(): quad_left = lax.all_gather(quad_slab, 'state', axis=1, tiled=True)  32.5 us
    another operation x4, other arithmetic, doubled(): both = jnp.stack([blocks, other])  13.8 us
    dot_general x2, matrix products, combine(): summed = jnp.dot(lead, trail, preferred_element_type=jnp.float32)  10.8 us
  transfers between devices with their start and end apart: 6, of which 6 were waited for; matrix products, arithmetic and copies ran while one was open for 1% of the time, Pallas kernels for 0%

profile of v1, /device:TPU:0, one launch (start us, length us, event | category | flops | bytes accessed | tf_op | source)
XLA Modules:
  0.0 421.0 jit_solution(12038492962052474470)
XLA Ops:
  6.5 0.0 copy-start.3
  6.5 0.0 copy-start.2
  6.5 0.0 all-gather.2.cloned.1.call-start
  7.2 2.9 copy.5
  10.2 0.0 copy-done.3
  10.2 0.0 copy-done.2
  10.2 3.4 fusion.4
  13.5 2.9 collective-permute-start
  16.5 90.9 %collective-permute-done = f32[2048,512]{0,1:T(8,128)} collective-permute-done((f32[2048,512]{0,1:T(8,128)}, f32[2048,512]{0,1:T(8,128)}, u32[]{:S(2)}, u32[]{:S(2)}) %collective-permute-start) | collective-permute-done | bytes 4194336 | tf_op jit(solution)/shard_map/ppermute | solution.py:28
  107.4 4.2 fusion.17
  111.5 0.0 collective-permute-start.1
  111.5 4.5 %collective-permute-done.1 = f32[1,1024,512]{1,2,0:T(8,128)} collective-permute-done((f32[1,1024,512]{1,2,0:T(8,128)}, f32[1,1024,512]{1,2,0:T(8,128)}, u32[]{:S(2)}, u32[]{:S(2)}) %collective-permute-start.1) | collective-permute-done | bytes 2097184 | tf_op jit(solution)/shard_map/ppermute | solution.py:20
  116.0 1.9 pad_maximum_fusion.1
  117.9 4.3 %fusion.6 = (f32[1,2,1024,512]{2,3,1,0:T(8,128)}, f32[2,1024,512]{1,2,0:T(8,128)}) fusion(f32[2,1,1024,512]{2,3,1,0:T(8,128)S(1)} %pad_maximum_fusion.1, pred[]{:T(512)S(6)} %eq.47), kind=kLoop, calls=%fused_computation.16 | loop fusion | flops 1048576 | bytes 12582913 | tf_op jit(solution)/shard_map/stack;reshape | solution.py:21
  122.2 1.8 collective-permute-start.2
  124.0 0.0 copy-start.1
  124.0 2.8 fusion.12
  126.8 88.4 %collective-permute-done.2 = f32[2,1024,512]{1,2,0:T(8,128)} collective-permute-done((f32[2,1024,512]{1,2,0:T(8,128)}, f32[2,1024,512]{1,2,0:T(8,128)}, u32[]{:S(2)}, u32[]{:S(2)}) %collective-permute-start.2) | collective-permute-done | bytes 4194336 | tf_op jit(solution)/shard_map/ppermute | solution.py:20
  215.2 0.0 copy-done.1
  215.2 3.4 pad_maximum_fusion
  218.6 1.2 fusion.30
  219.8 0.0 copy-start
  219.8 1.4 fusion.1
  221.2 0.8 copy-done
  222.0 4.8 %log_add_fusion = f32[1024,512]{0,1:T(8,128)S(1)} fusion(bf16[1024,2048]{0,1:T(8,128)(2,1)S(1)} %fusion.1, f32[512]{0:T(512)S(1)} %fusion.12, f32[2048,512]{0,1:T(8,128)} %collective-permute-done, f32[2048,512]{0,1:T(8,128)S(1)} %copy-done, pred[]{:T(512)S(6)} %eq.45, f32[1024]{0:T(1024)S(1)} %get-tuple-element.5), kind=kOutput, calls=%fused_computation.22 | convolution fusion | flops 2151677952 | bytes 14686209 | tf_op jit(solution)/shard_map/dot_general | solution.py:47
  226.8 0.1 collective-permute-start.3
  226.9 46.9 %collective-permute-done.3 = f32[1024,512]{0,1:T(8,128)S(1)} collective-permute-done((f32[1024,512]{0,1:T(8,128)S(1)}, f32[1024,512]{0,1:T(8,128)S(1)}, u32[]{:S(2)}, u32[]{:S(2)}) %collective-permute-start.3) | collective-permute-done | bytes 2097184 | tf_op jit(solution)/shard_map/ppermute | solution.py:28
  273.7 2.7 maximum_select_fusion
  276.5 1.8 collective-permute-start.4
  278.2 89.4 %collective-permute-done.4 = f32[2048,512]{0,1:T(8,128)} collective-permute-done((f32[2048,512]{0,1:T(8,128)}, f32[2048,512]{0,1:T(8,128)}, u32[]{:S(2)}, u32[]{:S(2)}) %collective-permute-start.4) | collective-permute-done | bytes 4194336 | tf_op jit(solution)/shard_map/ppermute | solution.py:28
  367.7 2.7 dynamic-slice_select_fusion.1
  370.4 0.0 all-gather.2.cloned.1.call-update
  370.4 2.6 fusion.13
  373.1 32.5 %all-gather.2.cloned.1.call-done = f32[512,2048]{0,1:T(8,128)} async-done(((f32[512,512]{0,1:T(8,128)}), f32[512,2048]{0,1:T(8,128)}) %all-gather.2.cloned.1.call-update) | async-done | bytes 4194320 | tf_op jit(solution)/shard_map/all_gather | solution.py:85
  405.6 2.5 reduce_max.38
  408.1 6.0 %add_add_fusion = f32[512,512]{1,0:T(8,128)} fusion(f32[512]{0:T(512)S(1)} %fusion.13, f32[512]{0:T(512)S(1)} %reduce_max.38, f32[2048,512]{0,1:T(8,128)} %collective-permute-done.4, f32[2048,512]{0,1:T(8,128)} %maximum_select_fusion, pred[]{:T(512)S(6)} %eq.44, f32[512,2048]{0,1:T(8,128)} %all-gather.2.cloned.1.call-done), kind=kOutput, calls=%fused_computation.30 | convolution fusion | flops 1079508992 | bytes 13635585 | tf_op jit(solution)/shard_map/dot_general | solution.py:47
  (2 shorter events, 0.0 us)
Async XLA Ops:
  6.5 3.6 copy-start.3
  6.5 3.6 copy-start.2
  6.5 399.0 %all-gather.2.cloned.1.call-start = ((), (), s32[]{:S(2)}) async-start(), calls=%async_computation | async-start | bytes 5242880 | tf_op jit(solution)/shard_map/all_gather | solution.py:85
  13.5 93.8 %collective-permute-start = (f32[2048,512]{0,1:T(8,128)}, f32[2048,512]{0,1:T(8,128)}, u32[]{:S(2)}, u32[]{:S(2)}) collective-permute-start(f32[2048,512]{0,1:T(8,128)} %fusion.4), channel_id=1, source_target_pairs={{0,4},{4,0},{8,12},{12,8},{16,20},{20,16},{24,28},{28,24},{1,5},{5... | collective-permute-start | bytes 12582920 | tf_op jit(solution)/shard_map/ppermute | solution.py:28
  111.5 4.5 %collective-permute-start.1 = (f32[1,1024,512]{1,2,0:T(8,128)}, f32[1,1024,512]{1,2,0:T(8,128)}, u32[]{:S(2)}, u32[]{:S(2)}) collective-permute-start(f32[1,1024,512]{1,2,0:T(8,128)} %get-tuple-element.8), channel_id=1, source_target_pairs={{0,1},{1,0},{2,3},{3,2},{4,5},{5,4},{6,7},{7,6},{8,9},{9,8},{10,11... | collective-permute-start | bytes 6291464 | tf_op jit(solution)/shard_map/ppermute | solution.py:20
  122.2 93.0 %collective-permute-start.2 = (f32[2,1024,512]{1,2,0:T(8,128)}, f32[2,1024,512]{1,2,0:T(8,128)}, u32[]{:S(2)}, u32[]{:S(2)}) collective-permute-start(f32[2,1024,512]{1,2,0:T(8,128)} %get-tuple-element.10), channel_id=1, source_target_pairs={{0,2},{1,3},{2,0},{3,1},{4,6},{5,7},{6,4},{7,5},{8,10},{9,11},{10,... | collective-permute-start | bytes 12582920 | tf_op jit(solution)/shard_map/ppermute | solution.py:20
  124.0 91.2 %copy-start.1 = (f32[1,2,1024,512]{2,3,1,0:T(8,128)S(1)}, f32[1,2,1024,512]{2,3,1,0:T(8,128)}, u32[]{:S(2)}) copy-start(f32[1,2,1024,512]{2,3,1,0:T(8,128)} %get-tuple-element.9) | copy-start | bytes 12582916
  219.8 2.2 copy-start
  226.8 46.9 %collective-permute-start.3 = (f32[1024,512]{0,1:T(8,128)S(1)}, f32[1024,512]{0,1:T(8,128)S(1)}, u32[]{:S(2)}, u32[]{:S(2)}) collective-permute-start(f32[1024,512]{0,1:T(8,128)S(1)} %log_add_fusion), channel_id=1, source_target_pairs={{0,4},{4,0},{8,12},{12,8},{16,20},{20,16},{24,28},{28,24},{1,5},{5... | collective-permute-start | bytes 6291464 | tf_op jit(solution)/shard_map/ppermute | solution.py:28
  276.5 91.2 %collective-permute-start.4 = (f32[2048,512]{0,1:T(8,128)}, f32[2048,512]{0,1:T(8,128)}, u32[]{:S(2)}, u32[]{:S(2)}) collective-permute-start(f32[2048,512]{0,1:T(8,128)} %maximum_select_fusion), channel_id=1, source_target_pairs={{0,8},{4,12},{8,0},{12,4},{16,24},{20,28},{24,16},{28,20},{1,9},{5... | collective-permute-start | bytes 12582920 | tf_op jit(solution)/shard_map/ppermute | solution.py:28
Sparse Core Ops, SparseCore 0:
  370.5 34.9 all-gather.1
